TPU v7x, 32 devices: a whole 2x2x4 slice. The times are simulated.
32 devices in a mesh: island: 8 (over y, x, core), fsdp: 4 (over z).
Axes of the slice: x: 2, y: 2, z: 4, core: 2. Of those that a mesh axis runs over, the one named last changes fastest.
Arguments:
- tokens: bfloat16 [8, 1024, 8192], P('island', 'fsdp'), may hold values from -6 to 6
- cotangent: bfloat16 [8, 1024, 1024], P('island', 'fsdp'), may hold values from -0.1875 to 0.1875
- params: float32 [8, 8192, 1024], P('island', 'fsdp'), may hold values from -0.18 to 0.18
- first_moment: bfloat16 [8, 8192, 1024], P('island', 'fsdp'), may hold values from -3 to 3
- second_moment: bfloat16 [8, 8192, 1024], P('island', 'fsdp'), may hold values from 0.25 to 4
- base: float32 [8192, 512], P(('fsdp', 'island')), may hold values from -0.18 to 0.18
- outer_momentum: float32 [8192, 512], P(('fsdp', 'island')), may hold values from -0.06 to 0.06
- head_order: int32 [8], replicated, may hold values from 0 to 7, each once
- step_fragment: int32 [1], replicated, may hold values from 0 to 1
Outputs:
- params_out: float32 [8, 8192, 1024], P('island', 'fsdp')
- first_out: bfloat16 [8, 8192, 1024], P('island', 'fsdp')
- second_out: bfloat16 [8, 8192, 1024], P('island', 'fsdp')
- base_out: float32 [8192, 512], P(('fsdp', 'island'))
- momentum_out: float32 [8192, 512], P(('fsdp', 'island'))
All inputs are finite; a program needn't handle non-finite values.
Results may differ from a plain program's by a relative error of at most 0.012.
Values may be sent and summed in bfloat16 or wider, within the bound.
No kernel may reach another device: no remote copies, remote signals or barrier semaphores. Data moves between devices by JAX's collectives and lax.ppermute only.
A program may use at most 128 MiB of HBM per device.

v0:
```python
import jax
import jax.numpy as jnp
from jax import lax
from jax.sharding import PartitionSpec as P

KVH = 8
HD = 128
SYNC = 4


def outer_update(base, outer_momentum, total, islands):
    delta = base - total / islands
    momentum = 0.9 * outer_momentum + delta
    return (base - 0.7 * (delta + 0.9 * momentum), momentum)


def shards(
    tokens,
    cotangent,
    params,
    first_moment,
    second_moment,
    base,
    outer_momentum,
    head_order,
    step_fragment,
):
    local_tokens = tokens[0]
    weights = params[0]
    rows = weights.shape[0]
    width = weights.shape[1]
    block = local_tokens.shape[0]
    columns = lax.all_to_all(tokens, "fsdp", split_axis=2, concat_axis=1, tiled=True)[0]
    piece = lax.all_gather(cotangent, "fsdp", axis=1, tiled=True)
    blocks = piece.shape[1] // block

    def one_block(index, running):
        grads_part = lax.dynamic_slice_in_dim(piece[0], index * block, block, 0)
        token_part = lax.dynamic_slice_in_dim(columns, index * block, block, 0)
        part = lax.dot_general(
            token_part, grads_part, (((0,), (0,)), ((), ())), preferred_element_type=jnp.float32
        )
        part = lax.optimization_barrier(part.astype(jnp.bfloat16)).astype(jnp.float32)
        return running + part

    grad = lax.fori_loop(0, blocks, one_block, jnp.zeros((rows, width), jnp.float32))
    moment_one = 0.9 * first_moment[0].astype(jnp.float32) + 0.1 * grad
    moment_two = 0.95 * second_moment[0].astype(jnp.float32) + 0.05 * grad * grad
    stepped = weights - 0.01 * (moment_one / (jnp.sqrt(moment_two) + 1e-08) + 0.1 * weights)
    heads = lax.dynamic_slice(head_order, (step_fragment[0] * SYNC,), (SYNC,))
    shaped = stepped.reshape(rows, KVH, HD)
    fragment = jnp.take(shaped, heads, axis=1).reshape(rows, SYNC * HD)
    islands = lax.axis_size("island")
    total = lax.psum_scatter(
        fragment.astype(jnp.bfloat16), "island", scatter_dimension=0, tiled=True
    ).astype(jnp.float32)
    base_next, momentum_next = outer_update(base, outer_momentum, total, islands)
    whole_base = lax.all_gather(
        base_next.astype(jnp.bfloat16), "island", axis=0, tiled=True
    ).astype(base_next.dtype)
    updated = shaped.at[:, heads, :].set(whole_base.reshape(rows, SYNC, HD)).reshape(rows, width)
    return (
        updated[None],
        moment_one.astype(jnp.bfloat16)[None],
        moment_two.astype(jnp.bfloat16)[None],
        base_next,
        momentum_next,
    )


def solution(mesh):
    placed = (
        P("island", "fsdp", None),
        P("island", "fsdp", None),
        P("island", "fsdp", None),
        P("island", "fsdp", None),
        P("island", "fsdp", None),
        P(("fsdp", "island"), None),
        P(("fsdp", "island"), None),
        P(),
        P(),
    )
    return jax.shard_map(
        shards,
        mesh=mesh,
        in_specs=placed,
        out_specs=(
            P("island", "fsdp", None),
            P("island", "fsdp", None),
            P("island", "fsdp", None),
            P(("fsdp", "island"), None),
            P(("fsdp", "island"), None),
        ),
        check_vma=False,
    )
```

profile of v0, /device:TPU:0, one launch (start us, length us, event | category | flops | bytes accessed | tf_op | source)
XLA Modules:
  0.0 422.3 jit_solution(16253507385062909303)
XLA Ops:
  7.2 17.8 %copy.73 = bf16[1,256,8192]{1,0,2:T(2,128)(2,1)} copy(bf16[1,256,8192]{2,1,0:T(8,128)(2,1)} %param.11) | data formatting | bytes 8388608 | tf_op args[0]
  24.9 0.5 broadcast.57
  25.4 43.5 %reduce = bf16[8192,256]{1,0:T(8,128)(2,1)} reduce(bf16[8192,1,256]{2,1,0:T(2,128)(2,1)} %bitcast.56, bf16[]{:T(256)} %broadcast.57), dimensions={1}, to_apply=%bitcast.50.reduce_sub_computation | reduce | bytes 8388610
  69.0 5.1 %reshape.62 = bf16[4,2,262144]{2,1,0:T(2,128)(2,1)} reshape(bf16[8192,256]{1,0:T(8,128)(2,1)} %reduce) | data formatting | bytes 8388608
  74.1 6.3 %all-to-all-start = ((bf16[4,2,262144]{2,1,0:T(2,128)(2,1)}), bf16[4,2,262144]{2,1,0:T(2,128)(2,1)}, u32[]{:S(2)}, u32[]{:S(2)}) async-start(bf16[4,2,262144]{2,1,0:T(2,128)(2,1)} %reshape.62), calls=%async_computation | async-start | bytes 8388608 | tf_op jit(solution)/shard_map/all_to_all | solution.py:33
  80.4 0.0 all-gather.3.cloned.1.call-start
  80.4 0.7 all-gather.3.cloned.1.call-update
  81.1 0.2 reduce-scatter.2.cloned.1.call-start
  82.0 9.3 %copy.71 = f32[1,2048,1024]{1,2,0:T(8,128)} copy(f32[1,2048,1024]{2,1,0:T(8,128)} %param.13) | data formatting | bytes 16777216 | tf_op args[2]
  91.3 0.0 copy-start.2
  91.3 6.6 %copy.72 = bf16[1,2048,1024]{1,2,0:T(8,128)(2,1)} copy(bf16[1,2048,1024]{2,1,0:T(8,128)(2,1)} %param.14) | data formatting | bytes 8388608 | tf_op args[3]
  97.9 6.5 %copy.76 = bf16[1,2048,1024]{1,2,0:T(8,128)(2,1)} copy(bf16[1,2048,1024]{2,1,0:T(8,128)(2,1)} %param.15) | data formatting | bytes 8388608 | tf_op args[4]
  104.4 0.0 copy-done.2
  104.4 0.1 compare_and_fusion
  104.5 0.1 broadcast_bitcast_fusion
  104.6 103.0 %all-to-all-done = bf16[4,2,262144]{2,1,0:T(2,128)(2,1)} async-done(((bf16[4,2,262144]{2,1,0:T(2,128)(2,1)}), bf16[4,2,262144]{2,1,0:T(2,128)(2,1)}, u32[]{:S(2)}, u32[]{:S(2)}) %all-to-all-start) | async-done | bytes 4194336 | tf_op jit(solution)/shard_map/all_to_all | solution.py:33
  207.6 7.4 %reshape.63 = bf16[8192,1,256]{2,1,0:T(2,128)(2,1)} reshape(bf16[4,2,262144]{2,1,0:T(2,128)(2,1)} %all-to-all-done) | data formatting | bytes 8388608
  215.0 6.1 %copy.90 = bf16[1,256,8192]{1,2,0:T(8,128)(2,1)} copy(bf16[1,256,8192]{1,0,2:T(2,128)(2,1)} %bitcast.57) | data formatting | bytes 8388608
  221.1 6.2 %copy.74 = bf16[1,4,256,2048]{3,2,1,0:T(8,128)(2,1)} copy(bf16[1,4,256,2048]{2,3,1,0:T(8,128)(2,1)} %bitcast.60) | data formatting | bytes 8388608 | tf_op jit(solution)/shard_map/all_to_all | solution.py:33
  227.3 0.0 all-gather.3.cloned.1.call-done
  227.3 57.0 %while.14 = (s32[]{:T(128)}, f32[2048,1024]{1,0:T(8,128)}, bf16[1024,2048]{1,0:T(8,128)(2,1)}, bf16[1,1024,1024]{2,1,0:T(8,128)(2,1)}, s32[]{:T(128)}, /*index=5*/s32[]{:T(128)}, s32[]{:T(128)}, s32[]{:T(128)}) while((s32[]{:T(128)}, f32[2048,1024]{1,0:T(8,128)}, bf16[1024,2048]{1,0:T(8,128)(2,1)}, ...), condition=%wide.region_1.0_spmd.clone, body=%wide.region_0.0_spmd.clone.sunk | while | flops 1082130432 | bytes 26739852 | solution.py:46
  227.3 4.7 %convolution_convert_fusion.2 = bf16[2048,1024]{1,0:T(8,128)(2,1)} fusion(bf16[1024,2048]{1,0:T(8,128)(2,1)} %get-tuple-element.179, s32[]{:T(128)S(6)} %select_n.32, bf16[1,1024,1024]{2,1,0:T(8,128)(2,1)} %get-tuple-element.180), kind=kOutput, calls=%fused_computation.3.clone.1 | convolution fusion | flops 1075838976 | bytes 5768192 | tf_op jit(solution)/shard_map/while/body/eval_jaxpr/dot_general | solution.py:40
  231.9 7.8 %select_add_fusion.2 = f32[2048,1024]{1,0:T(8,128)} fusion(f32[2048,1024]{1,0:T(8,128)} %get-tuple-element.170, bf16[2048,1024]{1,0:T(8,128)(2,1)} %convolution_convert_fusion.2, pred[]{:T(512)S(6)} %compare.3), kind=kLoop, calls=%fused_computation.2.clone.1 | loop fusion | flops 6291456 | bytes 20971520 | tf_op jit(solution)/shard_map/while/body/eval_jaxpr/add | solution.py:44
  239.7 4.7 %convolution_convert_fusion.2 = bf16[2048,1024]{1,0:T(8,128)(2,1)} fusion(bf16[1024,2048]{1,0:T(8,128)(2,1)} %get-tuple-element.179, s32[]{:T(128)S(6)} %select_n.32, bf16[1,1024,1024]{2,1,0:T(8,128)(2,1)} %get-tuple-element.180), kind=kOutput, calls=%fused_computation.3.clone.1 | convolution fusion | flops 1075838976 | bytes 5768192 | tf_op jit(solution)/shard_map/while/body/eval_jaxpr/dot_general | solution.py:40
  244.4 10.2 %select_add_fusion.2 = f32[2048,1024]{1,0:T(8,128)} fusion(f32[2048,1024]{1,0:T(8,128)} %get-tuple-element.170, bf16[2048,1024]{1,0:T(8,128)(2,1)} %convolution_convert_fusion.2, pred[]{:T(512)S(6)} %compare.3), kind=kLoop, calls=%fused_computation.2.clone.1 | loop fusion | flops 6291456 | bytes 20971520 | tf_op jit(solution)/shard_map/while/body/eval_jaxpr/add | solution.py:44
  254.6 4.7 %convolution_convert_fusion.2 = bf16[2048,1024]{1,0:T(8,128)(2,1)} fusion(bf16[1024,2048]{1,0:T(8,128)(2,1)} %get-tuple-element.179, s32[]{:T(128)S(6)} %select_n.32, bf16[1,1024,1024]{2,1,0:T(8,128)(2,1)} %get-tuple-element.180), kind=kOutput, calls=%fused_computation.3.clone.1 | convolution fusion | flops 1075838976 | bytes 5768192 | tf_op jit(solution)/shard_map/while/body/eval_jaxpr/dot_general | solution.py:40
  259.3 10.2 %select_add_fusion.2 = f32[2048,1024]{1,0:T(8,128)} fusion(f32[2048,1024]{1,0:T(8,128)} %get-tuple-element.170, bf16[2048,1024]{1,0:T(8,128)(2,1)} %convolution_convert_fusion.2, pred[]{:T(512)S(6)} %compare.3), kind=kLoop, calls=%fused_computation.2.clone.1 | loop fusion | flops 6291456 | bytes 20971520 | tf_op jit(solution)/shard_map/while/body/eval_jaxpr/add | solution.py:44
  269.5 4.7 %convolution_convert_fusion.2 = bf16[2048,1024]{1,0:T(8,128)(2,1)} fusion(bf16[1024,2048]{1,0:T(8,128)(2,1)} %get-tuple-element.179, s32[]{:T(128)S(6)} %select_n.32, bf16[1,1024,1024]{2,1,0:T(8,128)(2,1)} %get-tuple-element.180), kind=kOutput, calls=%fused_computation.3.clone.1 | convolution fusion | flops 1075838976 | bytes 5768192 | tf_op jit(solution)/shard_map/while/body/eval_jaxpr/dot_general | solution.py:40
  274.1 10.2 %select_add_fusion.2 = f32[2048,1024]{1,0:T(8,128)} fusion(f32[2048,1024]{1,0:T(8,128)} %get-tuple-element.170, bf16[2048,1024]{1,0:T(8,128)(2,1)} %convolution_convert_fusion.2, pred[]{:T(512)S(6)} %compare.3), kind=kLoop, calls=%fused_computation.2.clone.1 | loop fusion | flops 6291456 | bytes 20971520 | tf_op jit(solution)/shard_map/while/body/eval_jaxpr/add | solution.py:44
  284.3 9.2 %copy.75 = f32[2048,1024]{0,1:T(8,128)} copy(f32[2048,1024]{1,0:T(8,128)} %get-tuple-element.84) | data formatting | bytes 16777216 | tf_op jit(solution)/shard_map/while | solution.py:46
  293.5 15.2 %fusion.9 = (bf16[1,2048,1024]{1,2,0:T(8,128)(2,1)}, f32[2048,1024]{0,1:T(8,128)}, bf16[1,2048,1024]{1,2,0:T(8,128)(2,1)}) fusion(f32[2048,1024]{0,1:T(8,128)} %copy.75, bf16[1,2048,1024]{1,2,0:T(8,128)(2,1)} %copy.76, bf16[1,2048,1024]{1,2,0:T(8,128)(2,1)} %copy.72, f32[1,2048,1024]{1,2,0:T(8,128)} %copy.71), kind=kLoop, calls=%fused_computation.17 | loop fusion | flops 35651584 | bytes 41943040 | tf_op jit(solution)/shard_map/broadcast_in_dim | solution.py:65
  308.7 0.0 copy-start
  308.7 0.0 copy-start.1
  308.7 4.2 gather_fusion
  313.0 1.8 fusion.11
  314.7 0.0 reduce-scatter.2.cloned.1.call-update
  314.7 0.3 all-gather.5.cloned.1.call-start
  315.0 0.0 copy-done
  315.0 0.2 copy.80
  315.2 0.0 copy-done.1
  315.2 0.2 copy.81
  315.4 39.6 %reduce-scatter.2.cloned.1.call-done = bf16[256,512]{0,1:T(8,128)(2,1)} async-done(((bf16[2048,512]{0,1:T(8,128)(2,1)}), bf16[256,512]{0,1:T(8,128)(2,1)}) %reduce-scatter.2.cloned.1.call-update) | async-done | bytes 262160 | tf_op jit(solution)/shard_map/reduce_scatter | solution.py:54
  355.1 1.8 fusion.12
  356.9 0.0 all-gather.5.cloned.1.call-update
  356.9 9.2 %copy.83 = f32[2048,8,128]{2,0,1:T(8,128)} copy(f32[2048,8,128]{0,2,1:T(8,128)} %bitcast.55) | data formatting | bytes 16777216 | tf_op jit(solution)/shard_map/reshape | solution.py:51
  366.1 6.4 %copy.86 = bf16[1,2048,1024]{2,1,0:T(8,128)(2,1)} copy(bf16[1,2048,1024]{1,2,0:T(8,128)(2,1)} %get-tuple-element.134) | data formatting | bytes 8388608
  372.5 6.3 %copy.87 = bf16[1,2048,1024]{2,1,0:T(8,128)(2,1)} copy(bf16[1,2048,1024]{1,2,0:T(8,128)(2,1)} %get-tuple-element.132) | data formatting | bytes 8388608
  378.8 1.0 copy.88
  379.8 1.0 copy.89
  380.8 4.4 %all-gather.5.cloned.1.call-done = bf16[2048,512]{0,1:T(8,128)(2,1)} async-done(((bf16[256,512]{0,1:T(8,128)(2,1)}), bf16[2048,512]{0,1:T(8,128)(2,1)}) %all-gather.5.cloned.1.call-update) | async-done | bytes 2097168 | tf_op jit(solution)/shard_map/all_gather | solution.py:58
  385.2 4.1 copy.82
  389.3 8.1 %scatter_fusion = f32[2048,8,128]{2,0,1:T(8,128)} fusion(f32[2048,8,128]{2,0,1:T(8,128)} %copy.83, s32[4]{0:T(128)S(1)} %get-tuple-element.131, f32[4,2048,128]{2,1,0:T(8,128)} %bitcast.61), kind=kCustom, calls=%fused_computation.1 | custom fusion | bytes 12582928 | tf_op jit(solution)/shard_map/scatter | solution.py:61
  397.3 9.2 %copy.84 = f32[2048,8,128]{0,2,1:T(8,128)} copy(f32[2048,8,128]{2,0,1:T(8,128)} %scatter_fusion) | data formatting | bytes 16777216 | tf_op jit(solution)/shard_map/scatter | solution.py:61
  406.6 9.2 %copy.85 = f32[1,2048,1024]{2,1,0:T(8,128)} copy(f32[1,2048,1024]{1,2,0:T(8,128)} %bitcast.58) | data formatting | bytes 16777216
  (2 shorter events, 0.0 us)
Async XLA Ops:
  74.1 133.5 %all-to-all-start = ((bf16[4,2,262144]{2,1,0:T(2,128)(2,1)}), bf16[4,2,262144]{2,1,0:T(2,128)(2,1)}, u32[]{:S(2)}, u32[]{:S(2)}) async-start(bf16[4,2,262144]{2,1,0:T(2,128)(2,1)} %reshape.62), calls=%async_computation | async-start | bytes 8388608 | tf_op jit(solution)/shard_map/all_to_all | solution.py:33
  80.4 146.9 %all-gather.3.cloned.1.call-start = ((), (), s32[]{:S(2)}) async-start(), calls=%async_computation.2 | async-start | bytes 2621440 | tf_op jit(solution)/shard_map/all_gather | solution.py:34
  81.1 273.9 %reduce-scatter.2.cloned.1.call-start = ((), (), s32[]{:S(2)}) async-start(), calls=%async_computation.3 | async-start | bytes 2359296 | tf_op jit(solution)/shard_map/reduce_scatter | solution.py:54
  91.3 13.1 %copy-start.2 = (s32[8]{0:T(128)S(1)}, s32[8]{0:T(128)}, u32[]{:S(2)}) copy-start(s32[8]{0:T(128)} %param.18) | copy-start | bytes 100
  308.7 6.3 %copy-start = (f32[256,512]{1,0:T(8,128)S(1)}, f32[256,512]{1,0:T(8,128)}, u32[]{:S(2)}) copy-start(f32[256,512]{1,0:T(8,128)} %param.17) | copy-start | bytes 1572868
  308.7 6.5 %copy-start.1 = (f32[256,512]{1,0:T(8,128)S(1)}, f32[256,512]{1,0:T(8,128)}, u32[]{:S(2)}) copy-start(f32[256,512]{1,0:T(8,128)} %param.16) | copy-start | bytes 1572868
  314.7 70.4 %all-gather.5.cloned.1.call-start = ((), (), s32[]{:S(2)}) async-start(), calls=%async_computation.4 | async-start | bytes 2359296 | tf_op jit(solution)/shard_map/all_gather | solution.py:58
Sparse Core Ops, SparseCore 0:
  82.8 77.2 all-gather.2
  314.9 40.1 reduce-scatter.1
  357.1 28.0 all-gather.4
where the time goes:
time: 425 us; the launch traced here: 422 us
  waiting for transfers between devices  148 us (35%)
  local copies, waits for them, and re-layouts  134 us (32%)
  other arithmetic  101 us (24%)
  matrix products  18.6 us (4%)
  between operations  14.5 us (3%)
  starting transfers between devices  6.83 us (2%)
    all_to_all x1, waiting for transfers between devices, shards(): lax.all_to_all(tokens, 'fsdp', split_axis=2, concat_axis=1, tiled=True)[0]  103 us
    unnamed x21, local copies, waits for them, and re-layouts  83.5 us
    unnamed x2, other arithmetic  43.5 us
    reduce_scatter x1, waiting for transfers between devices, shards(): lax.psum_scatter(fragment.astype(jnp.bfloat16), 'island', scatter_dimensi...  39.6 us
    add x4, other arithmetic, one_block(): return running + part  38.4 us
    dot_general x4, matrix products, one_block(): lax.dot_general(token_part, grads_part, (((0,), (0,)), ((), ())), preferr...  18.6 us
    scatter x2, local copies, waits for them, and re-layouts, shards(): shaped.at[:, heads, :].set(whole_base.reshape(rows, SYNC, HD))  17.3 us
    broadcast_in_dim x1, other arithmetic, shards(): moment_two.astype(jnp.bfloat16)[None]  15.2 us
  transfers between devices with their start and end apart: 4, of which 3 were waited for; matrix products, arithmetic and copies ran while one was open for 16% of the time, Pallas kernels for 0%

commit v1 on v0

--- a/solution.py
+++ b/solution.py
@@ -30,7 +30,10 @@
     rows = weights.shape[0]
     width = weights.shape[1]
     block = local_tokens.shape[0]
-    columns = lax.all_to_all(tokens, "fsdp", split_axis=2, concat_axis=1, tiled=True)[0]
+    columns = jnp.concatenate(
+        lax.all_to_all(jnp.stack(jnp.split(tokens, lax.axis_size("fsdp"), axis=2)), "fsdp", 0, 0),
+        axis=1,
+    )[0]
     piece = lax.all_gather(cotangent, "fsdp", axis=1, tiled=True)
     blocks = piece.shape[1] // block
 

time: 425 us -> 343 us (0.81)
  other arithmetic: 101 us -> 59.6 us
  local copies, waits for them, and re-layouts: 134 us -> 93.4 us
    all_gather x1, waiting for transfers between devices: 0.01 us -> 55.7 us  [shards(): piece = lax.all_gather(cotangent, 'fsdp', axis=1, tiled=True)]
    all_to_all x1, waiting for transfers between devices: 103 us -> 47.5 us  [shards(): lax.all_to_all(jnp.stack(jnp.split(tokens, lax.axis_size('fsdp'), axis=2)...]
    unnamed x2 -> x1, other arithmetic: 43.5 us -> 0.01 us
    unnamed x21 -> x16, local copies, waits for them, and re-layouts: 83.5 us -> 46.6 us
    all_to_all x1 -> x0, local copies, waits for them, and re-layouts: 6.19 us -> none  [shards(): lax.all_to_all(tokens, 'fsdp', split_axis=2, concat_axis=1, tiled=True)[0]]
  transfers between devices with their start and end apart: 4 -> 4, of which waited for: 3 -> 4; matrix products, arithmetic and copies ran while one was open for 16% -> 14% of each run, Pallas kernels for 0% -> 0%
where the time goes in v1:
time: 343 us; the launch traced here: 341 us
  waiting for transfers between devices  148 us (43%)
  local copies, waits for them, and re-layouts  93.4 us (27%)
  other arithmetic  59.6 us (17%)
  matrix products  18.6 us (5%)
  between operations  14.5 us (4%)
  starting transfers between devices  6.61 us (2%)
    all_gather x1, waiting for transfers between devices, shards(): piece = lax.all_gather(cotangent, 'fsdp', axis=1, tiled=True)  55.7 us
    all_to_all x1, waiting for transfers between devices, shards(): lax.all_to_all(jnp.stack(jnp.split(tokens, lax.axis_size('fsdp'), axis=2)...  47.5 us
    unnamed x16, local copies, waits for them, and re-layouts  46.6 us
    reduce_scatter x1, waiting for transfers between devices, shards(): lax.psum_scatter(fragment.astype(jnp.bfloat16), 'island', scatter_dimensi...  39.8 us
    add x4, other arithmetic, one_block(): return running + part  38.4 us
    dot_general x4, matrix products, one_block(): lax.dot_general(token_part, grads_part, (((0,), (0,)), ((), ())), preferr...  18.6 us
    scatter x2, local copies, waits for them, and re-layouts, shards(): shaped.at[:, heads, :].set(whole_base.reshape(rows, SYNC, HD))  17.3 us
    broadcast_in_dim x1, other arithmetic, shards(): moment_two.astype(jnp.bfloat16)[None]  15.2 us
  transfers between devices with their start and end apart: 4, of which 4 were waited for; matrix products, arithmetic and copies ran while one was open for 14% of the time, Pallas kernels for 0%

profile of v1, /device:TPU:0, one launch (start us, length us, event | category | flops | bytes accessed | tf_op | source)
XLA Modules:
  0.0 340.9 jit_solution(6021229178864625108)
XLA Ops:
  7.2 2.8 slice_bitcast_fusion.3
  9.9 2.3 pad_maximum_fusion
  12.2 6.3 %all-to-all-start = ((bf16[4,1,256,2048]{3,2,1,0:T(8,128)(2,1)}), bf16[4,1,256,2048]{3,2,1,0:T(8,128)(2,1)}, u32[]{:S(2)}, u32[]{:S(2)}) async-start(bf16[4,1,256,2048]{3,2,1,0:T(8,128)(2,1)} %pad_maximum_fusion), calls=%async_computation | async-start | bytes 8388608 | tf_op jit(solution)/shard_map/all_to_all | solution.py:34
  18.6 0.0 all-gather.3.cloned.1.call-start
  18.6 0.7 all-gather.3.cloned.1.call-update
  19.3 0.0 reduce-scatter.2.cloned.1.call-start
  19.3 9.3 %copy.15 = f32[1,2048,1024]{1,2,0:T(8,128)} copy(f32[1,2048,1024]{2,1,0:T(8,128)} %param.13) | data formatting | bytes 16777216 | tf_op args[2]
  28.6 0.0 copy-start.2
  28.6 6.6 %copy.16 = bf16[1,2048,1024]{1,2,0:T(8,128)(2,1)} copy(bf16[1,2048,1024]{2,1,0:T(8,128)(2,1)} %param.14) | data formatting | bytes 8388608 | tf_op args[3]
  35.2 6.4 %copy.18 = bf16[1,2048,1024]{1,2,0:T(8,128)(2,1)} copy(bf16[1,2048,1024]{2,1,0:T(8,128)(2,1)} %param.15) | data formatting | bytes 8388608 | tf_op args[4]
  42.3 0.0 copy-done.2
  42.3 0.1 compare_and_fusion
  42.4 0.1 broadcast_bitcast_fusion
  42.5 55.7 %all-gather.3.cloned.1.call-done = bf16[1,1024,1024]{2,1,0:T(8,128)(2,1)} async-done(((bf16[1,256,1024]{2,1,0:T(8,128)(2,1)}), bf16[1,1024,1024]{2,1,0:T(8,128)(2,1)}) %all-gather.3.cloned.1.call-update) | async-done | bytes 2097168 | tf_op jit(solution)/shard_map/all_gather | solution.py:37
  98.2 47.5 %all-to-all-done = bf16[4,1,256,2048]{3,2,1,0:T(8,128)(2,1)} async-done(((bf16[4,1,256,2048]{3,2,1,0:T(8,128)(2,1)}), bf16[4,1,256,2048]{3,2,1,0:T(8,128)(2,1)}, u32[]{:S(2)}, u32[]{:S(2)}) %all-to-all-start) | async-done | bytes 4194336 | tf_op jit(solution)/shard_map/all_to_all | solution.py:34
  145.7 57.0 %while.14 = (s32[]{:T(128)}, f32[2048,1024]{1,0:T(8,128)}, bf16[1024,2048]{1,0:T(8,128)(2,1)}, bf16[1,1024,1024]{2,1,0:T(8,128)(2,1)}, s32[]{:T(128)}, /*index=5*/s32[]{:T(128)}, s32[]{:T(128)}, s32[]{:T(128)}) while((s32[]{:T(128)}, f32[2048,1024]{1,0:T(8,128)}, bf16[1024,2048]{1,0:T(8,128)(2,1)}, ...), condition=%wide.region_1.0_spmd.clone, body=%wide.region_0.0_spmd.clone.sunk | while | flops 1082130432 | bytes 26739852 | solution.py:49
  145.7 4.7 %convolution_convert_fusion.2 = bf16[2048,1024]{1,0:T(8,128)(2,1)} fusion(bf16[1024,2048]{1,0:T(8,128)(2,1)} %get-tuple-element.168, s32[]{:T(128)S(6)} %select_n.32, bf16[1,1024,1024]{2,1,0:T(8,128)(2,1)} %get-tuple-element.169), kind=kOutput, calls=%fused_computation.3.clone.1 | convolution fusion | flops 1075838976 | bytes 5768192 | tf_op jit(solution)/shard_map/while/body/eval_jaxpr/dot_general | solution.py:43
  150.4 7.8 %select_add_fusion.2 = f32[2048,1024]{1,0:T(8,128)} fusion(f32[2048,1024]{1,0:T(8,128)} %get-tuple-element.159, bf16[2048,1024]{1,0:T(8,128)(2,1)} %convolution_convert_fusion.2, pred[]{:T(512)S(6)} %compare.3), kind=kLoop, calls=%fused_computation.2.clone.1 | loop fusion | flops 6291456 | bytes 20971520 | tf_op jit(solution)/shard_map/while/body/eval_jaxpr/add | solution.py:47
  158.2 4.7 %convolution_convert_fusion.2 = bf16[2048,1024]{1,0:T(8,128)(2,1)} fusion(bf16[1024,2048]{1,0:T(8,128)(2,1)} %get-tuple-element.168, s32[]{:T(128)S(6)} %select_n.32, bf16[1,1024,1024]{2,1,0:T(8,128)(2,1)} %get-tuple-element.169), kind=kOutput, calls=%fused_computation.3.clone.1 | convolution fusion | flops 1075838976 | bytes 5768192 | tf_op jit(solution)/shard_map/while/body/eval_jaxpr/dot_general | solution.py:43
  162.8 10.2 %select_add_fusion.2 = f32[2048,1024]{1,0:T(8,128)} fusion(f32[2048,1024]{1,0:T(8,128)} %get-tuple-element.159, bf16[2048,1024]{1,0:T(8,128)(2,1)} %convolution_convert_fusion.2, pred[]{:T(512)S(6)} %compare.3), kind=kLoop, calls=%fused_computation.2.clone.1 | loop fusion | flops 6291456 | bytes 20971520 | tf_op jit(solution)/shard_map/while/body/eval_jaxpr/add | solution.py:47
  173.0 4.7 %convolution_convert_fusion.2 = bf16[2048,1024]{1,0:T(8,128)(2,1)} fusion(bf16[1024,2048]{1,0:T(8,128)(2,1)} %get-tuple-element.168, s32[]{:T(128)S(6)} %select_n.32, bf16[1,1024,1024]{2,1,0:T(8,128)(2,1)} %get-tuple-element.169), kind=kOutput, calls=%fused_computation.3.clone.1 | convolution fusion | flops 1075838976 | bytes 5768192 | tf_op jit(solution)/shard_map/while/body/eval_jaxpr/dot_general | solution.py:43
  177.7 10.2 %select_add_fusion.2 = f32[2048,1024]{1,0:T(8,128)} fusion(f32[2048,1024]{1,0:T(8,128)} %get-tuple-element.159, bf16[2048,1024]{1,0:T(8,128)(2,1)} %convolution_convert_fusion.2, pred[]{:T(512)S(6)} %compare.3), kind=kLoop, calls=%fused_computation.2.clone.1 | loop fusion | flops 6291456 | bytes 20971520 | tf_op jit(solution)/shard_map/while/body/eval_jaxpr/add | solution.py:47
  187.9 4.7 %convolution_convert_fusion.2 = bf16[2048,1024]{1,0:T(8,128)(2,1)} fusion(bf16[1024,2048]{1,0:T(8,128)(2,1)} %get-tuple-element.168, s32[]{:T(128)S(6)} %select_n.32, bf16[1,1024,1024]{2,1,0:T(8,128)(2,1)} %get-tuple-element.169), kind=kOutput, calls=%fused_computation.3.clone.1 | convolution fusion | flops 1075838976 | bytes 5768192 | tf_op jit(solution)/shard_map/while/body/eval_jaxpr/dot_general | solution.py:43
  192.5 10.2 %select_add_fusion.2 = f32[2048,1024]{1,0:T(8,128)} fusion(f32[2048,1024]{1,0:T(8,128)} %get-tuple-element.159, bf16[2048,1024]{1,0:T(8,128)(2,1)} %convolution_convert_fusion.2, pred[]{:T(512)S(6)} %compare.3), kind=kLoop, calls=%fused_computation.2.clone.1 | loop fusion | flops 6291456 | bytes 20971520 | tf_op jit(solution)/shard_map/while/body/eval_jaxpr/add | solution.py:47
  202.7 9.2 %copy.17 = f32[2048,1024]{0,1:T(8,128)} copy(f32[2048,1024]{1,0:T(8,128)} %get-tuple-element.84) | data formatting | bytes 16777216 | tf_op jit(solution)/shard_map/while | solution.py:49
  212.0 15.2 %fusion.9 = (bf16[1,2048,1024]{1,2,0:T(8,128)(2,1)}, f32[2048,1024]{0,1:T(8,128)}, bf16[1,2048,1024]{1,2,0:T(8,128)(2,1)}) fusion(f32[2048,1024]{0,1:T(8,128)} %copy.17, bf16[1,2048,1024]{1,2,0:T(8,128)(2,1)} %copy.18, bf16[1,2048,1024]{1,2,0:T(8,128)(2,1)} %copy.16, f32[1,2048,1024]{1,2,0:T(8,128)} %copy.15), kind=kLoop, calls=%fused_computation.17 | loop fusion | flops 35651584 | bytes 41943040 | tf_op jit(solution)/shard_map/broadcast_in_dim | solution.py:68
  227.2 0.0 copy-start
  227.2 0.0 copy-start.1
  227.2 4.2 %gather_fusion = bf16[4,2048,128]{1,2,0:T(8,128)(2,1)S(1)} fusion(f32[2048,8,128]{0,2,1:T(8,128)} %bitcast.57, s32[1024]{0:T(1024)S(1)} %pad_clamp_fusion), kind=kCustom, calls=%fused_computation | custom fusion | bytes 4194320 | tf_op jit(solution)/shard_map/jit(_take)/gather | solution.py:55
  231.4 1.8 fusion.11
  233.2 0.0 reduce-scatter.2.cloned.1.call-update
  233.2 0.2 all-gather.5.cloned.1.call-start
  233.4 0.0 copy-done
  233.4 0.2 copy.22
  233.6 0.0 copy-done.1
  233.6 0.2 copy.23
  233.8 39.8 %reduce-scatter.2.cloned.1.call-done = bf16[256,512]{0,1:T(8,128)(2,1)} async-done(((bf16[2048,512]{0,1:T(8,128)(2,1)}), bf16[256,512]{0,1:T(8,128)(2,1)}) %reduce-scatter.2.cloned.1.call-update) | async-done | bytes 262160 | tf_op jit(solution)/shard_map/reduce_scatter | solution.py:57
  273.7 1.8 fusion.12
  275.5 0.0 all-gather.5.cloned.1.call-update
  275.5 9.2 %copy.25 = f32[2048,8,128]{2,0,1:T(8,128)} copy(f32[2048,8,128]{0,2,1:T(8,128)} %bitcast.58) | data formatting | bytes 16777216 | tf_op jit(solution)/shard_map/reshape | solution.py:54
  284.7 6.4 %copy.28 = bf16[1,2048,1024]{2,1,0:T(8,128)(2,1)} copy(bf16[1,2048,1024]{1,2,0:T(8,128)(2,1)} %get-tuple-element.119) | data formatting | bytes 8388608
  291.1 6.3 %copy.29 = bf16[1,2048,1024]{2,1,0:T(8,128)(2,1)} copy(bf16[1,2048,1024]{1,2,0:T(8,128)(2,1)} %get-tuple-element.117) | data formatting | bytes 8388608
  297.4 1.0 copy.30
  298.4 1.0 copy.31
  299.4 4.4 %all-gather.5.cloned.1.call-done = bf16[2048,512]{0,1:T(8,128)(2,1)} async-done(((bf16[256,512]{0,1:T(8,128)(2,1)}), bf16[2048,512]{0,1:T(8,128)(2,1)}) %all-gather.5.cloned.1.call-update) | async-done | bytes 2097168 | tf_op jit(solution)/shard_map/all_gather | solution.py:61
  303.8 4.1 %copy.24 = f32[2048,4,128]{2,0,1:T(8,128)} copy(bf16[2048,4,128]{0,2,1:T(8,128)(2,1)} %bitcast.61) | data formatting | bytes 6291456 | tf_op jit(solution)/shard_map/reshape | solution.py:64
  307.9 8.0 %scatter_fusion = f32[2048,8,128]{2,0,1:T(8,128)} fusion(f32[2048,8,128]{2,0,1:T(8,128)} %copy.25, s32[4]{0:T(128)S(1)} %get-tuple-element.116, f32[4,2048,128]{2,1,0:T(8,128)} %bitcast.60), kind=kCustom, calls=%fused_computation.1 | custom fusion | bytes 12582928 | tf_op jit(solution)/shard_map/scatter | solution.py:64
  316.0 9.2 %copy.26 = f32[2048,8,128]{0,2,1:T(8,128)} copy(f32[2048,8,128]{2,0,1:T(8,128)} %scatter_fusion) | data formatting | bytes 16777216 | tf_op jit(solution)/shard_map/scatter | solution.py:64
  325.2 9.2 %copy.27 = f32[1,2048,1024]{2,1,0:T(8,128)} copy(f32[1,2048,1024]{1,2,0:T(8,128)} %bitcast.59) | data formatting | bytes 16777216
  (2 shorter events, 0.0 us)
Async XLA Ops:
  12.2 133.5 %all-to-all-start = ((bf16[4,1,256,2048]{3,2,1,0:T(8,128)(2,1)}), bf16[4,1,256,2048]{3,2,1,0:T(8,128)(2,1)}, u32[]{:S(2)}, u32[]{:S(2)}) async-start(bf16[4,1,256,2048]{3,2,1,0:T(8,128)(2,1)} %pad_maximum_fusion), calls=%async_computation | async-start | bytes 8388608 | tf_op jit(solution)/shard_map/all_to_all | solution.py:34
  18.6 79.7 %all-gather.3.cloned.1.call-start = ((), (), s32[]{:S(2)}) async-start(), calls=%async_computation.2 | async-start | bytes 2621440 | tf_op jit(solution)/shard_map/all_gather | solution.py:37
  19.3 254.4 %reduce-scatter.2.cloned.1.call-start = ((), (), s32[]{:S(2)}) async-start(), calls=%async_computation.3 | async-start | bytes 2359296 | tf_op jit(solution)/shard_map/reduce_scatter | solution.py:57
  28.6 13.7 %copy-start.2 = (s32[8]{0:T(128)S(1)}, s32[8]{0:T(128)}, u32[]{:S(2)}) copy-start(s32[8]{0:T(128)} %param.18) | copy-start | bytes 100
  227.2 6.2 %copy-start = (f32[256,512]{1,0:T(8,128)S(1)}, f32[256,512]{1,0:T(8,128)}, u32[]{:S(2)}) copy-start(f32[256,512]{1,0:T(8,128)} %param.17) | copy-start | bytes 1572868
  227.2 6.5 %copy-start.1 = (f32[256,512]{1,0:T(8,128)S(1)}, f32[256,512]{1,0:T(8,128)}, u32[]{:S(2)}) copy-start(f32[256,512]{1,0:T(8,128)} %param.16) | copy-start | bytes 1572868
  233.2 70.6 %all-gather.5.cloned.1.call-start = ((), (), s32[]{:S(2)}) async-start(), calls=%async_computation.4 | async-start | bytes 2359296 | tf_op jit(solution)/shard_map/all_gather | solution.py:61
Sparse Core Ops, SparseCore 0:
  20.9 77.2 all-gather.2
  233.3 40.3 reduce-scatter.1
  275.7 28.0 all-gather.4
